TPU v7x, 32 devices: a whole 2x2x4 slice. The times are simulated.
32 devices in a mesh: grp: 1, lat: 32 (over z, y, x, core).
Axes of the slice: x: 2, y: 2, z: 4, core: 2. Of those that a mesh axis runs over, the one named last changes fastest.
Arguments:
- fields: bfloat16 [768, 64, 2048], P(('grp', 'lat')), may hold values from -6 to 6
- spectral_weight: bfloat16 [2, 128, 64, 128], replicated, may hold values from -0.5 to 0.5
- local_weight: bfloat16 [2, 64, 64], replicated, may hold values from -0.75 to 0.75
Outputs:
- updated: bfloat16 [768, 64, 2048], P(('grp', 'lat'))
All inputs are finite; a program needn't handle non-finite values.
Results may differ from a plain program's by a relative error of at most 0.011.
Values may be sent and summed in bfloat16 or wider, within the bound.
A program may use at most 128 MiB of HBM per device.

v0:
```python
import functools
import math

import jax
import jax.numpy as jnp
import numpy as np
from jax import lax
from jax.experimental import pallas as pl
from jax.experimental.pallas import tpu as pltpu
from jax.sharding import PartitionSpec as P

KY = 128
MESH = pl.DeviceIdType.MESH
LAG = (0, 1, 4, 5, 8)
ROW_BLOCK = 8
CHUNK = 512


def lon_table(lon_count, mode_count):
    cells = np.arange(lon_count, dtype=np.int64)[:, None]
    modes = np.arange(mode_count, dtype=np.int64)[None, :]
    angle = (2.0 * np.pi / lon_count) * (cells * modes % lon_count)
    return np.stack([np.cos(angle), -np.sin(angle)], axis=1)


def lat_tables(devices, group, row_count, kept):
    lat_count = devices * row_count
    outer = devices // group
    index = np.arange(kept, dtype=np.int64)
    waves = np.where(index < kept // 2, index, lat_count - kept + index)
    device = np.arange(outer)[:, None, None] * group + np.arange(group)[None, :, None]
    latitudes = (np.arange(row_count)[None, None, :] * devices + device).reshape(outer, -1)
    angle = (2.0 * np.pi / lat_count) * (waves[None, :, None] * latitudes[:, None, :] % lat_count)
    both = np.concatenate([np.cos(angle), np.sin(angle)], axis=1) / math.sqrt(lat_count)
    turned = angle.transpose(0, 2, 1)
    back = np.concatenate([np.cos(turned), np.sin(turned)], axis=1) / math.sqrt(kept)
    return both, back


def lat_kernel(
    layer, group, outer, steps, rows, kept, channels,
    x_ref, weight_ref, fwd_ref, bwd_ref, y_ref,
    r_buf, p_buf, q_buf, m_buf, v_buf, fwd_buf, bwd_buf, w_buf, mix_buf, f_buf, acc, f_sem, g_sem,
    local_sem, w_sem, a_send, a_recv, b_send, b_recv, c_send, c_recv, d_send, d_recv,
):
    me = lax.axis_index("lat")
    z = me // group
    s = lax.rem(me, group)
    rows_all = rows * group

    def inner_peer(i):
        return lax.rem(s + i, group)

    def outer_peer(i):
        return lax.rem(z + i, outer)

    barrier = pltpu.get_barrier_semaphore()
    for i in range(1, group):
        pl.semaphore_signal(
            barrier, inc=1, device_id={"lat": z * group + inner_peer(i)}, device_id_type=MESH
        )
    for i in range(1, outer):
        pl.semaphore_signal(
            barrier, inc=1, device_id={"lat": outer_peer(i) * group + s}, device_id_type=MESH
        )

    def block(who):
        return pl.ds(pl.multiple_of(who * rows, 8), rows)

    def a_copy(t, i):
        to = inner_peer(i)
        return pltpu.make_async_remote_copy(
            src_ref=x_ref.at[pl.ds((to * steps + t) * outer, outer)],
            dst_ref=r_buf.at[t, :, block(s)],
            send_sem=a_send.at[t, i], recv_sem=a_recv.at[t, i],
            device_id={"lat": z * group + to}, device_id_type=MESH,
        )

    def b_copy(t, i):
        to = outer_peer(i)
        return pltpu.make_async_remote_copy(
            src_ref=p_buf.at[t, to], dst_ref=q_buf.at[t, z],
            send_sem=b_send.at[t, i], recv_sem=b_recv.at[t, i],
            device_id={"lat": to * group + s}, device_id_type=MESH,
        )

    def c_copy(t, i):
        to = outer_peer(i)
        return pltpu.make_async_remote_copy(
            src_ref=m_buf.at[t, z], dst_ref=m_buf.at[t, z],
            send_sem=c_send.at[t, i], recv_sem=c_recv.at[t, i],
            device_id={"lat": to * group + s}, device_id_type=MESH,
        )

    def d_copy(t, i):
        to = inner_peer(i)
        return pltpu.make_async_remote_copy(
            src_ref=v_buf.at[t, :, block(to)],
            dst_ref=y_ref.at[pl.ds((s * steps + t) * outer, outer)],
            send_sem=d_send.at[t, i], recv_sem=d_recv.at[t, i],
            device_id={"lat": z * group + to}, device_id_type=MESH,
        )

    def own_in(t):
        return pltpu.make_async_copy(
            x_ref.at[pl.ds((s * steps + t) * outer, outer)], r_buf.at[t, :, block(s)],
            local_sem.at[0, t],
        )

    def own_out(t):
        return pltpu.make_async_copy(
            v_buf.at[t, :, block(s)], y_ref.at[pl.ds((s * steps + t) * outer, outer)],
            local_sem.at[1, t],
        )

    def f_copy(t):
        return pltpu.make_async_remote_copy(
            src_ref=p_buf.at[t, outer - 1 - z], dst_ref=f_buf.at[t],
            send_sem=f_sem.at[0, t], recv_sem=f_sem.at[1, t],
            device_id={"lat": jnp.where(z == 0, 1, outer - 2) * group + s}, device_id_type=MESH,
        )

    def g_copy(t):
        block_of = outer_peer(2)
        return pltpu.make_async_remote_copy(
            src_ref=m_buf.at[t, block_of], dst_ref=m_buf.at[t, block_of],
            send_sem=g_sem.at[0, t], recv_sem=g_sem.at[1, t],
            device_id={"lat": (outer - 1 - block_of) * group + s}, device_id_type=MESH,
        )

    relay = outer == 4
    last = outer - 1
    at_end = jnp.logical_or(z == 0, z == last)
    inside = jnp.logical_not(at_end)

    fwd_copy = pltpu.make_async_copy(fwd_ref.at[z], fwd_buf, local_sem.at[0, steps])
    bwd_copy = pltpu.make_async_copy(bwd_ref.at[z], bwd_buf, local_sem.at[1, steps])
    w_copies = [
        pltpu.make_async_copy(
            weight_ref.at[layer, (s * steps + t) * outer + z], w_buf.at[t], w_sem.at[t]
        )
        for t in range(steps)
    ]
    fwd_copy.start()
    bwd_copy.start()
    for copy in w_copies:
        copy.start()
    for t in range(steps):
        own_in(t).start()
    pl.semaphore_wait(barrier, group - 1 + outer - 1)
    for t in range(steps):
        for i in range(1, group):
            a_copy(t, i).start()
    fwd_copy.wait()
    bwd_copy.wait()

    lane = lax.broadcasted_iota(jnp.int32, (1, 2 * channels), 1)
    fwd_sign = jnp.where(lane < channels, 1.0, -1.0).astype(jnp.float32)
    width = 2 * channels
    for t in range(steps):
        w_copies[t].wait()
        weight = w_buf[t].astype(jnp.float32)
        mix_buf[t, :channels] = w_buf[t]
        mix_buf[t, channels:] = (
            pltpu.roll(weight, channels, 1) * -fwd_sign
        ).astype(jnp.bfloat16)

    def forward(t):
        own_in(t).wait()
        for i in range(1, group):
            a_copy(t, i).wait_recv()
        for first in range(0, outer, 2):
            many = min(2, outer - first)
            pair = jnp.concatenate([r_buf[t, first + u] for u in range(many)], axis=1)
            both = jnp.dot(fwd_buf[...], pair, preferred_element_type=jnp.float32)
            for u in range(many):
                part = both[:, u * width:(u + 1) * width]
                out = part[:kept] + pltpu.roll(part[kept:], channels, 1) * fwd_sign
                p_buf[t, first + u] = out.astype(jnp.bfloat16)
        if not relay:
            for i in range(1, outer):
                b_copy(t, i).start()
            return
        pl.when(at_end)(lambda: f_copy(t).start())
        pl.when(at_end)(lambda: b_copy(t, 2).start())
        pl.when(z != last)(lambda: b_copy(t, 1).start())
        pl.when(z != 0)(lambda: b_copy(t, last).start())

    def relay_sum(t):
        if not relay:
            return

        @pl.when(inside)
        def _():
            f_copy(t).wait_recv()
            to = outer_peer(2)
            p_buf[t, to] = (
                p_buf[t, to].astype(jnp.float32) + f_buf[t].astype(jnp.float32)
            ).astype(jnp.bfloat16)
            b_copy(t, 2).start()

    def collect(t, i):
        b_copy(t, i).wait_recv()
        acc[...] += q_buf[t, lax.rem(z + outer - i, outer)].astype(jnp.float32)

    def middle(t):
        acc[...] = p_buf[t, z].astype(jnp.float32)
        if relay:
            pl.when(z != 0)(lambda: collect(t, 1))
            pl.when(z != last)(lambda: collect(t, last))
            collect(t, 2)
        else:
            for i in range(1, outer):
                collect(t, i)
        mixed = jnp.dot(
            acc[...].astype(jnp.bfloat16), mix_buf[t], preferred_element_type=jnp.float32
        )
        m_buf[t, z] = mixed.astype(jnp.bfloat16)
        if relay:
            c_copy(t, 2).start()
            pl.when(z != last)(lambda: c_copy(t, 1).start())
            pl.when(z != 0)(lambda: c_copy(t, last).start())
        else:
            for i in range(1, outer):
                c_copy(t, i).start()

    def relay_out(t):
        if not relay:
            return

        @pl.when(inside)
        def _():
            c_copy(t, 2).wait_recv()
            g_copy(t).start()

    def backward(t):
        if relay:
            pl.when(z != 0)(lambda: c_copy(t, 1).wait_recv())
            pl.when(z != last)(lambda: c_copy(t, last).wait_recv())
            pl.when(at_end)(lambda: c_copy(t, 2).wait_recv())
            pl.when(at_end)(lambda: g_copy(t).wait_recv())
        else:
            for i in range(1, outer):
                c_copy(t, i).wait_recv()
        for first in range(0, outer, 2):
            many = min(2, outer - first)
            pair = jnp.concatenate([m_buf[t, first + u] for u in range(many)], axis=1)
            both = jnp.dot(bwd_buf[...], pair, preferred_element_type=jnp.float32)
            for u in range(many):
                part = both[:, u * width:(u + 1) * width]
                out = part[:rows_all] - pltpu.roll(part[rows_all:], channels, 1) * fwd_sign
                v_buf[t, first + u] = out.astype(jnp.bfloat16)
        for i in range(1, group):
            d_copy(t, i).start()
        own_out(t).start()

    stages = tuple(zip((forward, relay_sum, middle, relay_out, backward), LAG))
    for step in range(steps + max(LAG)):
        for stage, lag in stages:
            if 0 <= step - lag < steps:
                stage(step - lag)

    for t in range(steps):
        own_out(t).wait()
        for i in range(1, group):
            d_copy(t, i).wait()
            a_copy(t, i).wait_send()
        if relay:
            pl.when(at_end)(lambda: f_copy(t).wait_send())
            pl.when(inside)(lambda: g_copy(t).wait_send())
            for copy in (b_copy, c_copy):
                copy(t, 2).wait_send()
                pl.when(z != last)(lambda: copy(t, 1).wait_send())
                pl.when(z != 0)(lambda: copy(t, last).wait_send())
        else:
            for i in range(1, outer):
                b_copy(t, i).wait_send()
                c_copy(t, i).wait_send()


def lat_part(x, weight, layer, forward_lat, backward_lat, devices, group):
    modes, rows, width = x.shape
    outer = devices // group
    steps = modes // devices
    kept = backward_lat.shape[2]
    dma = pltpu.SemaphoreType.DMA
    vmem = pl.BlockSpec(memory_space=pltpu.VMEM)
    hbm = pl.BlockSpec(memory_space=pl.ANY)
    return pl.pallas_call(
        functools.partial(lat_kernel, layer, group, outer, steps, rows, kept, width // 2),
        out_shape=jax.ShapeDtypeStruct(x.shape, jnp.bfloat16),
        in_specs=[vmem, hbm, hbm, hbm],
        out_specs=vmem,
        scratch_shapes=[
            pltpu.VMEM((steps, outer, rows * group, width), jnp.bfloat16),
            pltpu.VMEM((steps, outer, kept, width), jnp.bfloat16),
            pltpu.VMEM((steps, outer, kept, width), jnp.bfloat16),
            pltpu.VMEM((steps, outer, kept, width), jnp.bfloat16),
            pltpu.VMEM((steps, outer, rows * group, width), jnp.bfloat16),
            pltpu.VMEM(forward_lat.shape[1:], jnp.bfloat16),
            pltpu.VMEM(backward_lat.shape[1:], jnp.bfloat16),
            pltpu.VMEM((steps, width // 2, width), jnp.bfloat16),
            pltpu.VMEM((steps, width, width), jnp.bfloat16),
            pltpu.VMEM((steps, kept, width), jnp.bfloat16),
            pltpu.VMEM((kept, width), jnp.float32),
            dma((2, steps)), dma((2, steps)),
            dma((2, steps + 1)), dma((steps,)),
            dma((steps, group)), dma((steps, group)),
            dma((steps, outer)), dma((steps, outer)),
            dma((steps, outer)), dma((steps, outer)),
            dma((steps, group)), dma((steps, group)),
        ],
        compiler_params=pltpu.CompilerParams(collective_id=layer, has_side_effects=True),
        name="lat_part",
    )(x, weight, forward_lat, backward_lat)


def modes_out(flat, x_ref, turn):
    modes, rows, width = x_ref.shape
    channels = width // 2
    for n in range(rows):
        part = flat[n * channels:(n + 1) * channels]
        stacked = jnp.concatenate([part[:, :modes], part[:, modes:]], axis=0)
        turn[pl.ds(n, modes, stride=rows), :] = stacked.T
    x_ref[...] = turn[...].reshape(modes, rows, width).astype(jnp.bfloat16)


def lon_kernel(h_ref, table_ref, x_ref, turn):
    rows, channels, lon_count = h_ref.shape
    flat = jnp.dot(
        h_ref[...].reshape(rows * channels, lon_count), table_ref[...],
        preferred_element_type=jnp.float32,
    )
    modes_out(flat, x_ref, turn)


def field_kernel(layer, with_modes, y_ref, h_ref, back_ref, local_ref, *rest):
    if with_modes:
        table_ref, out_ref, x_ref, turn, turned, pointwise = rest
    else:
        out_ref, turn, turned, pointwise = rest
    modes, rows, width = y_ref.shape
    channels = width // 2
    lon_count = h_ref.shape[2]
    span = pointwise.shape[0] // channels

    @pl.when(pl.program_id(0) == 0)
    def _():
        pointwise[...] = jnp.zeros_like(pointwise)
        mixing = local_ref[layer].astype(jnp.float32).T.astype(jnp.bfloat16)
        for n in range(span):
            own = slice(n * channels, (n + 1) * channels)
            pointwise[own, own] = mixing

    turn[...] = y_ref[...].astype(jnp.float32).reshape(modes * rows, width)
    for n in range(rows):
        across = turn[pl.ds(n, modes, stride=rows), :].T
        turned[n * channels:(n + 1) * channels] = jnp.concatenate(
            [across[:channels], across[channels:]], axis=1
        ).astype(jnp.bfloat16)
    chunk = min(CHUNK, lon_count)
    inner = math.sqrt(2.0 / math.pi)
    for first in range(0, rows, span):
        many = span * channels
        spectrum = turned[first * channels:first * channels + many]
        for column in range(0, lon_count, chunk):
            cells = slice(column, column + chunk)
            total = jnp.dot(
                spectrum, back_ref[:, cells], preferred_element_type=jnp.float32
            ) + jnp.dot(
                pointwise[...], h_ref[first:first + span, :, cells].reshape(many, chunk),
                preferred_element_type=jnp.float32,
            )
            total = total.astype(jnp.bfloat16)
            curve = jnp.tanh(total * (inner + (inner * 0.044715) * (total * total)))
            out_ref[first:first + span, :, cells] = (
                (total * (0.5 + 0.5 * curve)).reshape(span, channels, chunk)
            )
    if with_modes:
        flat = jnp.dot(
            out_ref[...].reshape(rows * channels, lon_count), table_ref[...],
            preferred_element_type=jnp.float32,
        )
        modes_out(flat, x_ref, turn)


def whole_block(array):
    return pl.BlockSpec(array.shape, lambda i: (0,) * array.ndim, pipeline_mode=pl.Buffered(1))


def lon_part(h, table):
    rows, channels, lon_count = h.shape
    modes = table.shape[1] // 2
    width = 2 * channels
    return pl.pallas_call(
        lon_kernel,
        grid=(rows // ROW_BLOCK,),
        out_shape=jax.ShapeDtypeStruct((modes, rows, width), jnp.bfloat16),
        in_specs=[
            pl.BlockSpec((ROW_BLOCK, channels, lon_count), lambda i: (i, 0, 0)),
            whole_block(table),
        ],
        out_specs=pl.BlockSpec((modes, ROW_BLOCK, width), lambda i: (0, i, 0)),
        scratch_shapes=[pltpu.VMEM((modes * ROW_BLOCK, width), jnp.float32)],
        name="lon_part",
    )(h, table)


def field_part(y, h, back, local, layer, table=None):
    rows, channels, lon_count = h.shape
    modes, _, width = y.shape
    field = pl.BlockSpec((ROW_BLOCK, channels, lon_count), lambda i: (i, 0, 0))
    spectral = pl.BlockSpec((modes, ROW_BLOCK, width), lambda i: (0, i, 0))
    with_modes = table is not None
    many = max(1, min(ROW_BLOCK, 256 // channels)) * channels
    operands = [y, h, back, local] + ([table] if with_modes else [])
    shapes = [jax.ShapeDtypeStruct(h.shape, jnp.bfloat16)]
    if with_modes:
        shapes.append(jax.ShapeDtypeStruct(y.shape, jnp.bfloat16))
    out = pl.pallas_call(
        functools.partial(field_kernel, layer, with_modes),
        grid=(rows // ROW_BLOCK,),
        out_shape=shapes,
        in_specs=[spectral, field] + [whole_block(a) for a in operands[2:]],
        out_specs=[field, spectral][:len(shapes)],
        scratch_shapes=[
            pltpu.VMEM((modes * ROW_BLOCK, width), jnp.float32),
            pltpu.VMEM((ROW_BLOCK * channels, 2 * modes), jnp.bfloat16),
            pltpu.VMEM((many, many), jnp.bfloat16),
        ],
        name="field_part",
    )(*operands)
    return (out[0], out[1]) if with_modes else (out[0], None)


def shards(fields, spectral_weight, local_weight):
    row_count, channels, lon_count = fields.shape
    layer_count, mode_rows = spectral_weight.shape[:2]
    devices = lax.axis_size("lat")
    group = math.gcd(devices, 8)
    table = lon_table(lon_count, mode_rows)
    forward_lon = jnp.asarray(
        (table / math.sqrt(lon_count)).reshape(lon_count, 2 * mode_rows), jnp.bfloat16
    )
    backward_lon = jnp.asarray(
        (table.transpose(1, 2, 0) / math.sqrt(mode_rows)).reshape(2 * mode_rows, lon_count),
        jnp.bfloat16,
    )
    forward_all, backward_all = lat_tables(devices, group, row_count, KY)
    forward_lat = jnp.asarray(forward_all, jnp.bfloat16)
    backward_lat = jnp.asarray(backward_all, jnp.bfloat16)
    current = fields
    x = lon_part(current, forward_lon)
    for layer_idx in range(layer_count):
        y = lat_part(x, spectral_weight, layer_idx, forward_lat, backward_lat, devices, group)
        last_layer = layer_idx == layer_count - 1
        current, x = field_part(
            y, current, backward_lon, local_weight, layer_idx,
            None if last_layer else forward_lon,
        )
    return current


def solution(mesh):
    return jax.shard_map(
        shards,
        mesh=mesh,
        in_specs=(P(("grp", "lat"), None, None), P(), P()),
        out_specs=P(("grp", "lat"), None, None),
        check_vma=False,
    )
```

profile of v0, /device:TPU:0, one launch (start us, length us, event | category | flops | bytes accessed | tf_op | source)
XLA Modules:
  0.0 101.7 jit_solution(13085673578411569450)
XLA Ops:
  0.0 5.9 %lon_part.1.x_ref = bf16[128,24,128]{2,1,0:T(8,128)(2,1)} custom-call(bf16[24,64,2048]{2,1,0:T(8,128)(2,1)} %h_ref.3, bf16[2048,256]{1,0:T(8,128)(2,1)} %constant.8.clone.table_ref.rest_0_), custom_call_target="tpu_custom_call" | custom-call | tf_op jit(solution)/shard_map/lon_part/pallas_call | solution.py:395
  5.9 40.6 %lat_part.2.y_ref = bf16[128,24,128]{2,1,0:T(8,128)(2,1)} custom-call(bf16[128,24,128]{2,1,0:T(8,128)(2,1)} %lon_part.1.x_ref, bf16[2,128,64,128]{3,2,1,0:T(8,128)(2,1)} %weight_ref.3, bf16[4,256,192]{2,1,0:T(8,128)(2,1)} %constant.10.clone.fwd_ref, bf16[4,384,128]{2,1,0:T(8,128)(2,1)} %constant.11.clone.bwd_ref), custom_call_target="tpu_custom_call" | custom-call | tf_op jit(solution)/shard_map/lat_part/pallas_call | solution.py:289
  46.5 9.5 %field_part.2 = (bf16[24,64,2048]{2,1,0:T(8,128)(2,1)}, bf16[128,24,128]{2,1,0:T(8,128)(2,1)}) custom-call(bf16[128,24,128]{2,1,0:T(8,128)(2,1)} %lat_part.2.y_ref, bf16[24,64,2048]{2,1,0:T(8,128)(2,1)} %h_ref.3, bf16[256,2048]{1,0:T(8,128)(2,1)} %constant.9.clone.back_ref, bf16[2,64,64]{2,1,0:T(8,128)(2,1)} %local_ref.3, ...), custom_call_target="tpu_custom_call" | custom-call | tf_op jit(solution)/shard_map/field_part/pallas_call | solution.py:420
  56.0 36.9 %lat_part.3.y_ref = bf16[128,24,128]{2,1,0:T(8,128)(2,1)} custom-call(bf16[128,24,128]{2,1,0:T(8,128)(2,1)} %get-tuple-element.7.x_ref, bf16[2,128,64,128]{3,2,1,0:T(8,128)(2,1)} %weight_ref.3, bf16[4,256,192]{2,1,0:T(8,128)(2,1)} %constant.10.clone.fwd_ref, bf16[4,384,128]{2,1,0:T(8,128)(2,1)} %constant.11.clone.bwd_ref), custom_call_target="tpu_custom_call" | custom-call | tf_op jit(solution)/shard_map/lat_part/pallas_call | solution.py:289
  92.9 8.8 %field_part.3 = bf16[24,64,2048]{2,1,0:T(8,128)(2,1)} custom-call(bf16[128,24,128]{2,1,0:T(8,128)(2,1)} %lat_part.3.y_ref, bf16[24,64,2048]{2,1,0:T(8,128)(2,1)} %get-tuple-element.8.h_ref, bf16[256,2048]{1,0:T(8,128)(2,1)} %constant.9.clone.back_ref, bf16[2,64,64]{2,1,0:T(8,128)(2,1)} %local_ref.3), custom_call_target="tpu_custom_call" | custom-call | tf_op jit(solution)/shard_map/field_part/pallas_call | solution.py:420
where the time goes:
time: 102 us
  Pallas kernels  102 us (100%)
    pallas_call x2, Pallas kernels, lat_part(): pl.pallas_call(functools.partial(lat_kernel, layer, group, outer, steps,...  77.6 us
    pallas_call x2, Pallas kernels, field_part(): pl.pallas_call(functools.partial(field_kernel, layer, with_modes), grid=(...  18.2 us
    pallas_call x1, Pallas kernels, lon_part(): pl.pallas_call(lon_kernel, grid=(rows // ROW_BLOCK,), out_shape=jax.Shape...  5.9 us

commit v1 on v0

v1 whole, which is shorter than its diff:
```python
import functools
import math

import jax
import jax.numpy as jnp
import numpy as np
from jax import lax
from jax.experimental import pallas as pl
from jax.experimental.pallas import tpu as pltpu
from jax.sharding import PartitionSpec as P

KY = 128
MESH = pl.DeviceIdType.MESH
LAG = (0, 1, 4, 5, 8)
ROW_BLOCK = 8
CHUNK = 512


def lon_table(lon_count, mode_count):
    cells = np.arange(lon_count, dtype=np.int64)[:, None]
    modes = np.arange(mode_count, dtype=np.int64)[None, :]
    angle = (2.0 * np.pi / lon_count) * (cells * modes % lon_count)
    return np.stack([np.cos(angle), -np.sin(angle)], axis=1)


def lat_tables(devices, group, row_count, kept):
    lat_count = devices * row_count
    outer = devices // group
    index = np.arange(kept, dtype=np.int64)
    waves = np.where(index < kept // 2, index, lat_count - kept + index)
    plane = np.arange(outer)[:, None, None, None]
    row = np.arange(row_count).reshape(1, -1, 1, ROW_BLOCK)
    inner = np.arange(group)[None, None, :, None]
    latitudes = (row * devices + plane * group + inner).reshape(outer, -1)
    angle = (2.0 * np.pi / lat_count) * (waves[None, :, None] * latitudes[:, None, :] % lat_count)
    both = np.concatenate([np.cos(angle), np.sin(angle)], axis=2) / math.sqrt(lat_count)
    turned = angle.transpose(0, 2, 1)
    back = np.concatenate([np.cos(turned), -np.sin(turned)], axis=2) / math.sqrt(kept)
    return both, back


def modes_out(flat, turn):
    width = turn.shape[1]
    channels = width // 2
    rows = flat.shape[0] // channels
    modes = flat.shape[1] // 2
    for n in range(rows):
        part = flat[n * channels:(n + 1) * channels]
        stacked = jnp.concatenate([part[:, :modes], part[:, modes:]], axis=0)
        turn[pl.ds(n, modes, stride=rows), :] = stacked.T
    return turn[...].reshape(modes, rows, width).astype(jnp.bfloat16)


def block_mixing(local, pointwise):
    channels = local.shape[0]
    pointwise[...] = jnp.zeros_like(pointwise)
    mixing = (local.astype(jnp.float32).T * 0.5).astype(jnp.bfloat16)
    for n in range(pointwise.shape[0] // channels):
        own = slice(n * channels, (n + 1) * channels)
        pointwise[own, own] = mixing


def field_block(modes_in, h_ref, out_ref, back_ref, turn, turned, pointwise):
    modes, rows, width = modes_in.shape
    channels = width // 2
    lon_count = h_ref.shape[2]
    span = pointwise.shape[0] // channels
    turn[...] = modes_in.astype(jnp.float32).reshape(modes * rows, width)
    for n in range(rows):
        across = turn[pl.ds(n, modes, stride=rows), :].T
        turned[n * channels:(n + 1) * channels] = jnp.concatenate(
            [across[:channels], across[channels:]], axis=1
        ).astype(jnp.bfloat16)
    chunk = min(CHUNK, lon_count)
    inner = math.sqrt(2.0 / math.pi)
    for first in range(0, rows, span):
        many = span * channels
        spectrum = turned[first * channels:first * channels + many]
        for column in range(0, lon_count, chunk):
            cells = slice(column, column + chunk)
            half = jnp.dot(
                spectrum, back_ref[:, cells], preferred_element_type=jnp.float32
            ) + jnp.dot(
                pointwise[...], h_ref[first:first + span, :, cells].reshape(many, chunk),
                preferred_element_type=jnp.float32,
            )
            half = half.astype(jnp.bfloat16)
            curve = jnp.tanh(half * (2.0 * inner + (8.0 * inner * 0.044715) * (half * half)))
            out_ref[first:first + span, :, cells] = (
                (half * (1.0 + curve)).reshape(span, channels, chunk)
            )


def net_kernel(
    layers, group, outer, steps, order,
    h_ref, weight_ref, fwd_ref, bwd_ref, lon_ref, back_ref, local_ref, *rest,
):
    if layers > 1:
        y_ref, next_ref, *rest = rest
    else:
        y_ref, *rest = rest
    (
        h_buf, x_buf, r_buf, p_buf, q_buf, m_buf, v_buf, f_buf, acc,
        fwd_buf, bwd_buf, lon_buf, back_buf, w_buf, mix_buf, turn, turned, pointwise,
        h_sem, next_sem, table_sem, w_sem, own_in_sem, own_out_sem, f_sem, g_sem,
        a_send, a_recv, b_send, b_recv, c_send, c_recv, d_send, d_recv,
    ) = rest
    chunks, block, channels, lon_count = h_buf.shape
    modes, width = x_buf.shape[1], x_buf.shape[3]
    held = steps * outer
    kept = p_buf.shape[2]
    tall = chunks * group * block
    me = lax.axis_index("lat")
    z = me // group
    s = lax.rem(me, group)

    def inner_peer(i):
        return lax.rem(s + i, group)

    def outer_peer(i):
        return lax.rem(z + i, outer)

    h_copies = [
        pltpu.make_async_copy(h_ref.at[pl.ds(i * block, block)], h_buf.at[i], h_sem.at[i])
        for i in range(chunks)
    ]
    lon_copy = pltpu.make_async_copy(lon_ref, lon_buf, table_sem.at[0])
    back_copy = pltpu.make_async_copy(back_ref, back_buf, table_sem.at[1])
    fwd_copy = pltpu.make_async_copy(fwd_ref.at[z], fwd_buf, table_sem.at[2])
    bwd_copy = pltpu.make_async_copy(bwd_ref.at[z], bwd_buf, table_sem.at[3])
    w_copies = [
        pltpu.make_async_copy(
            weight_ref.at[l, (s * steps + t) * outer + z], w_buf.at[l, t], w_sem.at[l, t]
        )
        for l in range(layers) for t in range(steps)
    ]
    h_copies[0].start()
    lon_copy.start()
    for copy in h_copies[1:]:
        copy.start()

    barrier = pltpu.get_barrier_semaphore()
    for i in range(1, group):
        pl.semaphore_signal(
            barrier, inc=1, device_id={"lat": z * group + inner_peer(i)}, device_id_type=MESH
        )
    for i in range(1, outer):
        pl.semaphore_signal(
            barrier, inc=1, device_id={"lat": outer_peer(i) * group + s}, device_id_type=MESH
        )
    fwd_copy.start()
    bwd_copy.start()
    for copy in w_copies:
        copy.start()
    back_copy.start()

    parts = [(0, 1, 0, held)] if chunks > 1 else []
    first_tail = len(parts)
    parts += [(first_tail, chunks - first_tail, t * outer, outer) for t in range(steps)]

    def a_copy(part, i):
        to = inner_peer(i)
        c0, nc, m0, nm = parts[part]
        return pltpu.make_async_remote_copy(
            src_ref=x_buf.at[pl.ds(c0, nc), pl.ds(to * held + m0, nm)],
            dst_ref=r_buf.at[pl.ds(c0, nc), s, pl.ds(m0, nm)],
            send_sem=a_send.at[part, i], recv_sem=a_recv.at[part, i],
            device_id={"lat": z * group + to}, device_id_type=MESH,
        )

    def own_in(part):
        c0, nc, m0, nm = parts[part]
        return pltpu.make_async_copy(
            x_buf.at[pl.ds(c0, nc), pl.ds(s * held + m0, nm)],
            r_buf.at[pl.ds(c0, nc), s, pl.ds(m0, nm)],
            own_in_sem.at[part],
        )

    def b_copy(t, i):
        to = outer_peer(i)
        return pltpu.make_async_remote_copy(
            src_ref=p_buf.at[t, to], dst_ref=q_buf.at[t, z],
            send_sem=b_send.at[t, i], recv_sem=b_recv.at[t, i],
            device_id={"lat": to * group + s}, device_id_type=MESH,
        )

    def c_copy(t, i):
        to = outer_peer(i)
        return pltpu.make_async_remote_copy(
            src_ref=m_buf.at[t, z], dst_ref=m_buf.at[t, z],
            send_sem=c_send.at[t, i], recv_sem=c_recv.at[t, i],
            device_id={"lat": to * group + s}, device_id_type=MESH,
        )

    def d_copy(slot, c0, nc, t, i):
        to = inner_peer(i)
        return pltpu.make_async_remote_copy(
            src_ref=v_buf.at[pl.ds(c0, nc), to, pl.ds(t * outer, outer)],
            dst_ref=y_ref.at[pl.ds(c0, nc), pl.ds((s * steps + t) * outer, outer)],
            send_sem=d_send.at[slot, i], recv_sem=d_recv.at[slot, i],
            device_id={"lat": z * group + to}, device_id_type=MESH,
        )

    def own_out(slot, c0, nc, t):
        return pltpu.make_async_copy(
            v_buf.at[pl.ds(c0, nc), s, pl.ds(t * outer, outer)],
            y_ref.at[pl.ds(c0, nc), pl.ds((s * steps + t) * outer, outer)],
            own_out_sem.at[slot],
        )

    d_parts = [(t, 0, chunks, t) for t in range(steps - 1)]
    d_parts += [(steps - 1 + c, c, 1, steps - 1) for c in range(chunks)]

    def f_copy(t):
        return pltpu.make_async_remote_copy(
            src_ref=p_buf.at[t, outer - 1 - z], dst_ref=f_buf.at[t],
            send_sem=f_sem.at[0, t], recv_sem=f_sem.at[1, t],
            device_id={"lat": jnp.where(z == 0, 1, outer - 2) * group + s}, device_id_type=MESH,
        )

    def g_copy(t):
        block_of = outer_peer(2)
        return pltpu.make_async_remote_copy(
            src_ref=m_buf.at[t, block_of], dst_ref=m_buf.at[t, block_of],
            send_sem=g_sem.at[0, t], recv_sem=g_sem.at[1, t],
            device_id={"lat": (outer - 1 - block_of) * group + s}, device_id_type=MESH,
        )

    relay = outer == 4
    last = outer - 1
    at_end = jnp.logical_or(z == 0, z == last)
    inside = jnp.logical_not(at_end)
    lane = lax.broadcasted_iota(jnp.int32, (1, width), 1)
    sign = jnp.where(lane < channels, 1.0, -1.0)

    def swapped(values):
        return (pltpu.roll(values.astype(jnp.float32), channels, 1) * sign).astype(jnp.bfloat16)

    def lon_block(i):
        flat = jnp.dot(
            h_buf[i].reshape(block * channels, lon_count), lon_buf[...],
            preferred_element_type=jnp.float32,
        )
        x_buf[i] = modes_out(flat, turn)

    def send_part(part):
        own_in(part).start()
        for i in range(1, group):
            a_copy(part, i).start()

    def send_head(i):
        if first_tail:
            pl.when(i == 0)(lambda: send_part(0))

    def send_tail():
        for part in range(first_tail, len(parts)):
            send_part(part)

    def forward(t):
        for part in ([0] if t == 0 and first_tail else []) + [first_tail + t]:
            own_in(part).wait()
            for i in range(1, group):
                a_copy(part, i).wait_recv()
        for first in range(0, outer, 2):
            pair = []
            for u in range(first, min(first + 2, outer)):
                values = r_buf[:, :, t * outer + u].reshape(tall, width)
                pair.append(jnp.concatenate([values, swapped(values)], axis=0))
            out = jnp.dot(
                fwd_buf[...], jnp.concatenate(pair, axis=1), preferred_element_type=jnp.float32
            ).astype(jnp.bfloat16)
            for u in range(len(pair)):
                p_buf[t, first + u] = out[:, u * width:(u + 1) * width]
        if not relay:
            for i in range(1, outer):
                b_copy(t, i).start()
            return
        pl.when(at_end)(lambda: f_copy(t).start())
        pl.when(at_end)(lambda: b_copy(t, 2).start())
        pl.when(z != last)(lambda: b_copy(t, 1).start())
        pl.when(z != 0)(lambda: b_copy(t, last).start())

    def relay_sum(t):
        if not relay:
            return

        @pl.when(inside)
        def _():
            f_copy(t).wait_recv()
            to = outer_peer(2)
            p_buf[t, to] = (
                p_buf[t, to].astype(jnp.float32) + f_buf[t].astype(jnp.float32)
            ).astype(jnp.bfloat16)
            b_copy(t, 2).start()

    def collect(t, i):
        b_copy(t, i).wait_recv()
        acc[...] += q_buf[t, lax.rem(z + outer - i, outer)].astype(jnp.float32)

    def middle(t):
        acc[...] = p_buf[t, z].astype(jnp.float32)
        if relay:
            pl.when(z != 0)(lambda: collect(t, 1))
            pl.when(z != last)(lambda: collect(t, last))
            collect(t, 2)
        else:
            for i in range(1, outer):
                collect(t, i)
        mixed = jnp.dot(
            acc[...].astype(jnp.bfloat16), mix_buf[t], preferred_element_type=jnp.float32
        )
        m_buf[t, z] = mixed.astype(jnp.bfloat16)
        if relay:
            c_copy(t, 2).start()
            pl.when(z != last)(lambda: c_copy(t, 1).start())
            pl.when(z != 0)(lambda: c_copy(t, last).start())
        else:
            for i in range(1, outer):
                c_copy(t, i).start()

    def relay_out(t):
        if not relay:
            return

        @pl.when(inside)
        def _():
            c_copy(t, 2).wait_recv()
            g_copy(t).start()

    def backward(t):
        if relay:
            pl.when(z != 0)(lambda: c_copy(t, 1).wait_recv())
            pl.when(z != last)(lambda: c_copy(t, last).wait_recv())
            pl.when(at_end)(lambda: c_copy(t, 2).wait_recv())
            pl.when(at_end)(lambda: g_copy(t).wait_recv())
        else:
            for i in range(1, outer):
                c_copy(t, i).wait_recv()
        for first in range(0, outer, 2):
            pair = []
            for u in range(first, min(first + 2, outer)):
                values = m_buf[t, u]
                pair.append(jnp.concatenate([values, swapped(values)], axis=0))
            out = jnp.dot(
                bwd_buf[...], jnp.concatenate(pair, axis=1), preferred_element_type=jnp.float32
            ).astype(jnp.bfloat16)
            for u in range(len(pair)):
                v_buf[:, :, t * outer + first + u] = out[:, u * width:(u + 1) * width].reshape(
                    chunks, group, block, width
                )
        for slot, c0, nc, _ in [p for p in d_parts if p[3] == t]:
            for i in range(1, group):
                d_copy(slot, c0, nc, t, i).start()
            own_out(slot, c0, nc, t).start()

    def landed(slot, c0, nc, t):
        own_out(slot, c0, nc, t).wait()
        for i in range(1, group):
            d_copy(slot, c0, nc, t, i).wait_recv()

    def lat_sent():
        for part in range(len(parts)):
            for i in range(1, group):
                a_copy(part, i).wait_send()
        for t in range(steps):
            if relay:
                pl.when(at_end)(lambda: f_copy(t).wait_send())
                pl.when(inside)(lambda: g_copy(t).wait_send())
                for copy in (b_copy, c_copy):
                    copy(t, 2).wait_send()
                    pl.when(z != last)(lambda: copy(t, 1).wait_send())
                    pl.when(z != 0)(lambda: copy(t, last).wait_send())
            else:
                for i in range(1, outer):
                    b_copy(t, i).wait_send()
                    c_copy(t, i).wait_send()

    def back_sent():
        for slot, c0, nc, t in d_parts:
            for i in range(1, group):
                d_copy(slot, c0, nc, t, i).wait_send()

    stages = {
        "forward": forward, "relay_sum": relay_sum, "middle": middle,
        "relay_out": relay_out, "backward": backward,
    }

    def lat_block(layer):
        for t in range(steps):
            weight = w_buf[layer, t].astype(jnp.float32)
            mix_buf[t, :channels] = w_buf[layer, t]
            mix_buf[t, channels:] = (
                pltpu.roll(weight, channels, 1) * -sign
            ).astype(jnp.bfloat16)
        for name, t in order:
            stages[name](t)
        for part in d_parts[:steps - 1]:
            landed(*part)
        lat_sent()

    def next_copy(i):
        return pltpu.make_async_copy(
            h_buf.at[i], next_ref.at[pl.ds(i * block, block)], next_sem.at[i]
        )

    h_copies[0].wait()
    lon_copy.wait()

    @pl.loop(0, chunks)
    def _(i):
        lon_block(i)

        @pl.when(i == 0)
        def _():
            pl.semaphore_wait(barrier, group - 1 + outer - 1)
            for copy in h_copies[1:]:
                copy.wait()
        send_head(i)

    send_tail()
    fwd_copy.wait()
    bwd_copy.wait()
    for copy in w_copies:
        copy.wait()
    back_copy.wait()

    @pl.loop(0, layers)
    def _(layer):
        lat_block(layer)

        @pl.when(layer < layers - 1)
        def _():
            block_mixing(local_ref[layer], pointwise)

            @pl.loop(0, chunks)
            def _(i):
                landed(steps - 1 + i, i, 1, steps - 1)
                field_block(
                    y_ref[i], h_buf.at[i], h_buf.at[i], back_buf, turn, turned, pointwise
                )
                pl.when(layer == layers - 2)(lambda: next_copy(i).start())
                lon_block(i)
                send_head(i)

        @pl.when(layer == layers - 1)
        def _():
            for part in d_parts[steps - 1:]:
                landed(*part)
        back_sent()
        pl.when(layer < layers - 1)(send_tail)

    if layers > 1:
        for i in range(chunks):
            next_copy(i).wait()


def schedule(steps, lags):
    names = ("forward", "relay_sum", "middle", "relay_out", "backward")
    return [
        (name, step - lag)
        for step in range(steps + max(lags))
        for name, lag in zip(names, lags)
        if 0 <= step - lag < steps
    ]


def net_part(h, weight, fwd, bwd, lon, back, local, devices, group):
    rows, channels, lon_count = h.shape
    layers, modes, _, width = weight.shape
    outer = devices // group
    steps = modes // devices
    chunks = rows // ROW_BLOCK
    kept = fwd.shape[1]
    held = steps * outer
    dma = pltpu.SemaphoreType.DMA
    vmem = pl.BlockSpec(memory_space=pltpu.VMEM)
    hbm = pl.BlockSpec(memory_space=pl.ANY)
    bf16 = jnp.bfloat16
    many = max(1, min(ROW_BLOCK, 256 // channels)) * channels
    shapes = [jax.ShapeDtypeStruct((chunks, modes, ROW_BLOCK, width), bf16)]
    if layers > 1:
        shapes.append(jax.ShapeDtypeStruct(h.shape, bf16))
    part_count = steps + (1 if chunks > 1 else 0)
    slots = steps - 1 + chunks
    out = pl.pallas_call(
        functools.partial(net_kernel, layers, group, outer, steps, schedule(steps, LAG)),
        out_shape=shapes,
        in_specs=[hbm] * 6 + [vmem],
        out_specs=[vmem, hbm][:len(shapes)],
        scratch_shapes=[
            pltpu.VMEM((chunks, ROW_BLOCK, channels, lon_count), bf16),
            pltpu.VMEM((chunks, modes, ROW_BLOCK, width), bf16),
            pltpu.VMEM((chunks, group, held, ROW_BLOCK, width), bf16),
            pltpu.VMEM((steps, outer, kept, width), bf16),
            pltpu.VMEM((steps, outer, kept, width), bf16),
            pltpu.VMEM((steps, outer, kept, width), bf16),
            pltpu.VMEM((chunks, group, held, ROW_BLOCK, width), bf16),
            pltpu.VMEM((steps, kept, width), bf16),
            pltpu.VMEM((kept, width), jnp.float32),
            pltpu.VMEM(fwd.shape[1:], bf16),
            pltpu.VMEM(bwd.shape[1:], bf16),
            pltpu.VMEM(lon.shape, bf16),
            pltpu.VMEM(back.shape, bf16),
            pltpu.VMEM((layers, steps, channels, width), bf16),
            pltpu.VMEM((steps, width, width), bf16),
            pltpu.VMEM((modes * ROW_BLOCK, width), jnp.float32),
            pltpu.VMEM((ROW_BLOCK * channels, 2 * modes), bf16),
            pltpu.VMEM((many, many), bf16),
            dma((chunks,)), dma((chunks,)), dma((4,)), dma((layers, steps)),
            dma((part_count,)), dma((slots,)), dma((2, steps)), dma((2, steps)),
            dma((part_count, group)), dma((part_count, group)),
            dma((steps, outer)), dma((steps, outer)),
            dma((steps, outer)), dma((steps, outer)),
            dma((slots, group)), dma((slots, group)),
        ],
        compiler_params=pltpu.CompilerParams(collective_id=0, has_side_effects=True),
        name="net_part",
    )(h, weight, fwd, bwd, lon, back, local)
    return out[0], (out[1] if layers > 1 else h)


def field_kernel(layer, y_ref, h_ref, back_ref, local_ref, out_ref, turn, turned, pointwise):
    @pl.when(pl.program_id(0) == 0)
    def _():
        block_mixing(local_ref[layer], pointwise)

    field_block(y_ref[0], h_ref, out_ref, back_ref, turn, turned, pointwise)


def whole_block(array):
    return pl.BlockSpec(array.shape, lambda i: (0,) * array.ndim, pipeline_mode=pl.Buffered(1))


def field_part(y, h, back, local, layer):
    rows, channels, lon_count = h.shape
    _, modes, _, width = y.shape
    field = pl.BlockSpec((ROW_BLOCK, channels, lon_count), lambda i: (i, 0, 0))
    spectral = pl.BlockSpec((1, modes, ROW_BLOCK, width), lambda i: (i, 0, 0, 0))
    many = max(1, min(ROW_BLOCK, 256 // channels)) * channels
    return pl.pallas_call(
        functools.partial(field_kernel, layer),
        grid=(rows // ROW_BLOCK,),
        out_shape=jax.ShapeDtypeStruct(h.shape, jnp.bfloat16),
        in_specs=[spectral, field, whole_block(back), whole_block(local)],
        out_specs=field,
        scratch_shapes=[
            pltpu.VMEM((modes * ROW_BLOCK, width), jnp.float32),
            pltpu.VMEM((ROW_BLOCK * channels, 2 * modes), jnp.bfloat16),
            pltpu.VMEM((many, many), jnp.bfloat16),
        ],
        name="field_part",
    )(y, h, back, local)


def shards(fields, spectral_weight, local_weight):
    row_count, channels, lon_count = fields.shape
    layer_count, mode_rows = spectral_weight.shape[:2]
    devices = lax.axis_size("lat")
    group = math.gcd(devices, 8)
    table = lon_table(lon_count, mode_rows)
    forward_lon = jnp.asarray(
        (table / math.sqrt(lon_count)).reshape(lon_count, 2 * mode_rows), jnp.bfloat16
    )
    backward_lon = jnp.asarray(
        (table.transpose(1, 2, 0) * (0.5 / math.sqrt(mode_rows))).reshape(
            2 * mode_rows, lon_count
        ),
        jnp.bfloat16,
    )
    forward_all, backward_all = lat_tables(devices, group, row_count, KY)
    forward_lat = jnp.asarray(forward_all, jnp.bfloat16)
    backward_lat = jnp.asarray(backward_all, jnp.bfloat16)
    y, h = net_part(
        fields, spectral_weight, forward_lat, backward_lat, forward_lon, backward_lon,
        local_weight, devices, group,
    )
    return field_part(y, h, backward_lon, local_weight, layer_count - 1)


def solution(mesh):
    return jax.shard_map(
        shards,
        mesh=mesh,
        in_specs=(P(("grp", "lat"), None, None), P(), P()),
        out_specs=P(("grp", "lat"), None, None),
        check_vma=False,
    )
```

time: 102 us -> 89.1 us (0.87)
  Pallas kernels: 102 us -> 88.8 us
    pallas_call x5 -> x2, Pallas kernels: 102 us -> 88.8 us  [the longest x1 80 us: net_part(): pl.pallas_call(functools.partial(net_kernel, layers, group, outer, steps,...]
where the time goes in v1:
time: 89.1 us; the launch traced here: 88.8 us
  Pallas kernels  88.8 us (100%)
    pallas_call x1, Pallas kernels, net_part(): pl.pallas_call(functools.partial(net_kernel, layers, group, outer, steps,...  80 us
    pallas_call x1, Pallas kernels, field_part(): pl.pallas_call(functools.partial(field_kernel, layer), grid=(rows // ROW_...  8.8 us

profile of v1, /device:TPU:0, one launch (start us, length us, event | category | flops | bytes accessed | tf_op | source)
XLA Modules:
  0.0 88.8 jit_solution(2770947524503967502)
XLA Ops:
  0.0 80.0 %net_part.1 = (bf16[3,128,8,128]{3,2,1,0:T(8,128)(2,1)}, bf16[24,64,2048]{2,1,0:T(8,128)(2,1)}) custom-call(bf16[24,64,2048]{2,1,0:T(8,128)(2,1)} %h_ref.1, bf16[2,128,64,128]{3,2,1,0:T(8,128)(2,1)} %weight_ref.1, bf16[4,128,384]{2,1,0:T(8,128)(2,1)} %constant.10.clone.fwd_ref, bf16[4,192,256]{2,1,0:T(8,128)(2,1)} %constant.11.clone.bwd_ref, ...), custom_call_target="tpu_custom_call" | custom-call | tf_op jit(solution)/shard_map/net_part/pallas_call | solution.py:485
  80.0 8.8 %field_part.1 = bf16[24,64,2048]{2,1,0:T(8,128)(2,1)} custom-call(bf16[3,128,8,128]{3,2,1,0:T(8,128)(2,1)} %get-tuple-element.7.y_ref, bf16[24,64,2048]{2,1,0:T(8,128)(2,1)} %get-tuple-element.8.h_ref, bf16[256,2048]{1,0:T(8,128)(2,1)} %constant.9.clone.back_ref, bf16[2,64,64]{2,1,0:T(8,128)(2,1)} %local_ref.3), custom_call_target="tpu_custom_call" | custom-call | tf_op jit(solution)/shard_map/field_part/pallas_call | solution.py:540

commit v2 on v1

--- a/solution.py
+++ b/solution.py
@@ -14,6 +14,8 @@
 LAG = (0, 1, 4, 5, 8)
 ROW_BLOCK = 8
 CHUNK = 512
+NET_VMEM = 20 << 20
+FIELD_VMEM = 8 << 20
 
 
 def lon_table(lon_count, mode_count):
@@ -60,51 +62,59 @@
         pointwise[own, own] = mixing
 
 
-def field_block(modes_in, h_ref, out_ref, back_ref, turn, turned, pointwise):
+def pointwise_block(h_ref, out_ref, pointwise):
+    rows, channels, lon_count = h_ref.shape
+    many = pointwise.shape[0]
+    span = many // channels
+    chunk = min(CHUNK, lon_count)
+    for first in range(0, rows, span):
+        for column in range(0, lon_count, chunk):
+            cells = slice(column, column + chunk)
+            out_ref[first * channels:first * channels + many, cells] = jnp.dot(
+                pointwise[...], h_ref[first:first + span, :, cells].reshape(many, chunk),
+                preferred_element_type=jnp.float32,
+            )
+
+
+def spectrum_block(modes_in, turn, turned):
     modes, rows, width = modes_in.shape
     channels = width // 2
-    lon_count = h_ref.shape[2]
-    span = pointwise.shape[0] // channels
     turn[...] = modes_in.astype(jnp.float32).reshape(modes * rows, width)
     for n in range(rows):
         across = turn[pl.ds(n, modes, stride=rows), :].T
         turned[n * channels:(n + 1) * channels] = jnp.concatenate(
             [across[:channels], across[channels:]], axis=1
         ).astype(jnp.bfloat16)
+
+
+def field_rows(first, span, local_ref, out_ref, back_ref, turned):
+    _, channels, lon_count = out_ref.shape
     chunk = min(CHUNK, lon_count)
     inner = math.sqrt(2.0 / math.pi)
-    for first in range(0, rows, span):
-        many = span * channels
-        spectrum = turned[first * channels:first * channels + many]
-        for column in range(0, lon_count, chunk):
-            cells = slice(column, column + chunk)
-            half = jnp.dot(
-                spectrum, back_ref[:, cells], preferred_element_type=jnp.float32
-            ) + jnp.dot(
-                pointwise[...], h_ref[first:first + span, :, cells].reshape(many, chunk),
-                preferred_element_type=jnp.float32,
-            )
-            half = half.astype(jnp.bfloat16)
-            curve = jnp.tanh(half * (2.0 * inner + (8.0 * inner * 0.044715) * (half * half)))
-            out_ref[first:first + span, :, cells] = (
-                (half * (1.0 + curve)).reshape(span, channels, chunk)
-            )
+    own = slice(first * channels, (first + span) * channels)
+    for column in range(0, lon_count, chunk):
+        cells = slice(column, column + chunk)
+        half = local_ref[own, cells] + jnp.dot(
+            turned[own], back_ref[:, cells], preferred_element_type=jnp.float32
+        )
+        half = half.astype(jnp.bfloat16)
+        curve = jnp.tanh(half * (2.0 * inner + (8.0 * inner * 0.044715) * (half * half)))
+        out_ref[first:first + span, :, cells] = (
+            (half * (1.0 + curve)).reshape(span, channels, chunk)
+        )
 
 
 def net_kernel(
     layers, group, outer, steps, order,
-    h_ref, weight_ref, fwd_ref, bwd_ref, lon_ref, back_ref, local_ref, *rest,
+    h_ref, weight_ref, fwd_ref, bwd_ref, lon_ref, back_ref, mixing_ref, *rest,
 ):
-    if layers > 1:
-        y_ref, next_ref, *rest = rest
-    else:
-        y_ref, *rest = rest
     (
-        h_buf, x_buf, r_buf, p_buf, q_buf, m_buf, v_buf, f_buf, acc,
-        fwd_buf, bwd_buf, lon_buf, back_buf, w_buf, mix_buf, turn, turned, pointwise,
-        h_sem, next_sem, table_sem, w_sem, own_in_sem, own_out_sem, f_sem, g_sem,
+        y_ref, pw_buf, back_buf, h_buf, x_buf, r_buf, p_buf, q_buf, m_buf, v_buf, f_buf, acc,
+        fwd_buf, bwd_buf, lon_buf, local_ref, w_buf, mix_buf, turn, turned, pointwise,
+        h_sem, table_sem, w_sem, own_in_sem, own_out_sem, f_sem, g_sem,
         a_send, a_recv, b_send, b_recv, c_send, c_recv, d_send, d_recv,
     ) = rest
+    span = pointwise.shape[0] // h_buf.shape[2]
     chunks, block, channels, lon_count = h_buf.shape
     modes, width = x_buf.shape[1], x_buf.shape[3]
     held = steps * outer
@@ -125,6 +135,7 @@
         for i in range(chunks)
     ]
     lon_copy = pltpu.make_async_copy(lon_ref, lon_buf, table_sem.at[0])
+    local_copy = pltpu.make_async_copy(mixing_ref, local_ref, table_sem.at[4])
     back_copy = pltpu.make_async_copy(back_ref, back_buf, table_sem.at[1])
     fwd_copy = pltpu.make_async_copy(fwd_ref.at[z], fwd_buf, table_sem.at[2])
     bwd_copy = pltpu.make_async_copy(bwd_ref.at[z], bwd_buf, table_sem.at[3])
@@ -148,6 +159,7 @@
         pl.semaphore_signal(
             barrier, inc=1, device_id={"lat": outer_peer(i) * group + s}, device_id_type=MESH
         )
+    local_copy.start()
     fwd_copy.start()
     bwd_copy.start()
     for copy in w_copies:
@@ -392,16 +404,17 @@
             mix_buf[t, channels:] = (
                 pltpu.roll(weight, channels, 1) * -sign
             ).astype(jnp.bfloat16)
+        block_mixing(local_ref[layer], pointwise)
+
+        @pl.loop(0, chunks)
+        def _(i):
+            pointwise_block(h_buf.at[i], pw_buf.at[i], pointwise)
+
         for name, t in order:
             stages[name](t)
         for part in d_parts[:steps - 1]:
             landed(*part)
         lat_sent()
-
-    def next_copy(i):
-        return pltpu.make_async_copy(
-            h_buf.at[i], next_ref.at[pl.ds(i * block, block)], next_sem.at[i]
-        )
 
     h_copies[0].wait()
     lon_copy.wait()
@@ -418,6 +431,7 @@
         send_head(i)
 
     send_tail()
+    local_copy.wait()
     fwd_copy.wait()
     bwd_copy.wait()
     for copy in w_copies:
@@ -430,15 +444,12 @@
 
         @pl.when(layer < layers - 1)
         def _():
-            block_mixing(local_ref[layer], pointwise)
-
             @pl.loop(0, chunks)
             def _(i):
                 landed(steps - 1 + i, i, 1, steps - 1)
-                field_block(
-                    y_ref[i], h_buf.at[i], h_buf.at[i], back_buf, turn, turned, pointwise
-                )
-                pl.when(layer == layers - 2)(lambda: next_copy(i).start())
+                spectrum_block(y_ref[i], turn, turned)
+                for first in range(0, block, span):
+                    field_rows(first, span, pw_buf.at[i], h_buf.at[i], back_buf, turned)
                 lon_block(i)
                 send_head(i)
 
@@ -448,10 +459,6 @@
                 landed(*part)
         back_sent()
         pl.when(layer < layers - 1)(send_tail)
-
-    if layers > 1:
-        for i in range(chunks):
-            next_copy(i).wait()
 
 
 def schedule(steps, lags):
@@ -474,19 +481,25 @@
     held = steps * outer
     dma = pltpu.SemaphoreType.DMA
     vmem = pl.BlockSpec(memory_space=pltpu.VMEM)
-    hbm = pl.BlockSpec(memory_space=pl.ANY)
+    hbm = pl.BlockSpec(memory_space=pltpu.HBM)
     bf16 = jnp.bfloat16
     many = max(1, min(ROW_BLOCK, 256 // channels)) * channels
-    shapes = [jax.ShapeDtypeStruct((chunks, modes, ROW_BLOCK, width), bf16)]
-    if layers > 1:
-        shapes.append(jax.ShapeDtypeStruct(h.shape, bf16))
+    shapes = [
+        jax.ShapeDtypeStruct((chunks, modes, ROW_BLOCK, width), bf16),
+        jax.ShapeDtypeStruct((chunks, ROW_BLOCK * channels, lon_count), jnp.float32),
+        jax.ShapeDtypeStruct(back.shape, bf16),
+    ]
     part_count = steps + (1 if chunks > 1 else 0)
     slots = steps - 1 + chunks
-    out = pl.pallas_call(
+    operands = [
+        pltpu.with_memory_space_constraint(a, pltpu.HBM)
+        for a in (h, weight, fwd, bwd, lon, back, local)
+    ]
+    return pl.pallas_call(
         functools.partial(net_kernel, layers, group, outer, steps, schedule(steps, LAG)),
         out_shape=shapes,
-        in_specs=[hbm] * 6 + [vmem],
-        out_specs=[vmem, hbm][:len(shapes)],
+        in_specs=[hbm] * 7,
+        out_specs=[vmem] * 3,
         scratch_shapes=[
             pltpu.VMEM((chunks, ROW_BLOCK, channels, lon_count), bf16),
             pltpu.VMEM((chunks, modes, ROW_BLOCK, width), bf16),
@@ -500,56 +513,72 @@
             pltpu.VMEM(fwd.shape[1:], bf16),
             pltpu.VMEM(bwd.shape[1:], bf16),
             pltpu.VMEM(lon.shape, bf16),
-            pltpu.VMEM(back.shape, bf16),
+            pltpu.VMEM(local.shape, bf16),
             pltpu.VMEM((layers, steps, channels, width), bf16),
             pltpu.VMEM((steps, width, width), bf16),
             pltpu.VMEM((modes * ROW_BLOCK, width), jnp.float32),
             pltpu.VMEM((ROW_BLOCK * channels, 2 * modes), bf16),
             pltpu.VMEM((many, many), bf16),
-            dma((chunks,)), dma((chunks,)), dma((4,)), dma((layers, steps)),
+            dma((chunks,)), dma((5,)), dma((layers, steps)),
             dma((part_count,)), dma((slots,)), dma((2, steps)), dma((2, steps)),
             dma((part_count, group)), dma((part_count, group)),
             dma((steps, outer)), dma((steps, outer)),
             dma((steps, outer)), dma((steps, outer)),
             dma((slots, group)), dma((slots, group)),
         ],
-        compiler_params=pltpu.CompilerParams(collective_id=0, has_side_effects=True),
+        compiler_params=pltpu.CompilerParams(
+            collective_id=0, has_side_effects=True, vmem_limit_bytes=NET_VMEM
+        ),
         name="net_part",
-    )(h, weight, fwd, bwd, lon, back, local)
-    return out[0], (out[1] if layers > 1 else h)
-
-
-def field_kernel(layer, y_ref, h_ref, back_ref, local_ref, out_ref, turn, turned, pointwise):
-    @pl.when(pl.program_id(0) == 0)
-    def _():
-        block_mixing(local_ref[layer], pointwise)
-
-    field_block(y_ref[0], h_ref, out_ref, back_ref, turn, turned, pointwise)
-
-
-def whole_block(array):
-    return pl.BlockSpec(array.shape, lambda i: (0,) * array.ndim, pipeline_mode=pl.Buffered(1))
-
-
-def field_part(y, h, back, local, layer):
-    rows, channels, lon_count = h.shape
-    _, modes, _, width = y.shape
-    field = pl.BlockSpec((ROW_BLOCK, channels, lon_count), lambda i: (i, 0, 0))
-    spectral = pl.BlockSpec((1, modes, ROW_BLOCK, width), lambda i: (i, 0, 0, 0))
-    many = max(1, min(ROW_BLOCK, 256 // channels)) * channels
+    )(*operands)
+
+
+def field_kernel(y_ref, local_ref, back_ref, out_ref, turned, turn, out_buf, out_sem):
+    chunks, modes, rows, width = y_ref.shape
+    channels = width // 2
+    span = out_buf.shape[1]
+    pieces = [(i, first) for i in range(chunks) for first in range(0, rows, span)]
+
+    def out_copy(k):
+        i, first = pieces[k]
+        return pltpu.make_async_copy(
+            out_buf.at[k % 2], out_ref.at[pl.ds(i * rows + first, span)], out_sem.at[k % 2]
+        )
+
+    for k, (i, first) in enumerate(pieces):
+        if first == 0:
+            spectrum_block(y_ref[i], turn, turned)
+        if k >= 2:
+            out_copy(k - 2).wait()
+        own = slice(first * channels, (first + span) * channels)
+        field_rows(
+            0, span, local_ref.at[i, own], out_buf.at[k % 2], back_ref, turned.at[own]
+        )
+        out_copy(k).start()
+    for k in range(max(0, len(pieces) - 2), len(pieces)):
+        out_copy(k).wait()
+
+
+def field_part(y, local, back):
+    chunks, modes, rows, width = y.shape
+    channels = width // 2
+    lon_count = back.shape[1]
+    span = max(1, min(rows, 256 // channels))
+    vmem = pl.BlockSpec(memory_space=pltpu.VMEM)
     return pl.pallas_call(
-        functools.partial(field_kernel, layer),
-        grid=(rows // ROW_BLOCK,),
-        out_shape=jax.ShapeDtypeStruct(h.shape, jnp.bfloat16),
-        in_specs=[spectral, field, whole_block(back), whole_block(local)],
-        out_specs=field,
+        field_kernel,
+        out_shape=jax.ShapeDtypeStruct((chunks * rows, channels, lon_count), jnp.bfloat16),
+        in_specs=[vmem] * 3,
+        out_specs=pl.BlockSpec(memory_space=pltpu.HBM),
         scratch_shapes=[
-            pltpu.VMEM((modes * ROW_BLOCK, width), jnp.float32),
-            pltpu.VMEM((ROW_BLOCK * channels, 2 * modes), jnp.bfloat16),
-            pltpu.VMEM((many, many), jnp.bfloat16),
+            pltpu.VMEM((rows * channels, 2 * modes), jnp.bfloat16),
+            pltpu.VMEM((modes * rows, width), jnp.float32),
+            pltpu.VMEM((2, span, channels, lon_count), jnp.bfloat16),
+            pltpu.SemaphoreType.DMA((2,)),
         ],
+        compiler_params=pltpu.CompilerParams(vmem_limit_bytes=FIELD_VMEM),
         name="field_part",
-    )(y, h, back, local)
+    )(y, local, back)
 
 
 def shards(fields, spectral_weight, local_weight):
@@ -570,11 +599,11 @@
     forward_all, backward_all = lat_tables(devices, group, row_count, KY)
     forward_lat = jnp.asarray(forward_all, jnp.bfloat16)
     backward_lat = jnp.asarray(backward_all, jnp.bfloat16)
-    y, h = net_part(
+    y, local, back = net_part(
         fields, spectral_weight, forward_lat, backward_lat, forward_lon, backward_lon,
         local_weight, devices, group,
     )
-    return field_part(y, h, backward_lon, local_weight, layer_count - 1)
+    return field_part(y, local, back)
 
 
 def solution(mesh):

time: 89.1 us -> 83.4 us (0.936)
  Pallas kernels: 88.8 us -> 83.2 us
    pallas_call x1, Pallas kernels: 8.8 us -> 5.62 us  [field_part(): pl.pallas_call(field_kernel, out_shape=jax.ShapeDtypeStruct((chunks * row...]
    pallas_call x1, Pallas kernels: 80 us -> 77.6 us  [net_part(): pl.pallas_call(functools.partial(net_kernel, layers, group, outer, steps,...]
where the time goes in v2:
time: 83.4 us; the launch traced here: 83.2 us
  Pallas kernels  83.2 us (100%)
    pallas_call x1, Pallas kernels, net_part(): pl.pallas_call(functools.partial(net_kernel, layers, group, outer, steps,...  77.6 us
    pallas_call x1, Pallas kernels, field_part(): pl.pallas_call(field_kernel, out_shape=jax.ShapeDtypeStruct((chunks * row...  5.62 us

profile of v2, /device:TPU:0, one launch (start us, length us, event | category | flops | bytes accessed | tf_op | source)
XLA Modules:
  0.0 83.2 jit_solution(16504760412458754057)
XLA Ops:
  0.0 77.6 %net_part.1 = (bf16[3,128,8,128]{3,2,1,0:T(8,128)(2,1)S(1)}, f32[3,512,2048]{2,1,0:T(8,128)S(1)}, bf16[256,2048]{1,0:T(8,128)(2,1)S(1)}) custom-call(bf16[24,64,2048]{2,1,0:T(8,128)(2,1)} %h_ref.1, bf16[2,128,64,128]{3,2,1,0:T(8,128)(2,1)} %weight_ref.1, bf16[4,128,384]{2,1,0:T(8,128)(2,1)} %constant.10.clone.fwd_ref, ...), custom_call_target="tpu_custom_call" | custom-call | tf_op jit(solution)/shard_map/net_part/pallas_call | solution.py:498
  77.6 5.6 %field_part.1 = bf16[24,64,2048]{2,1,0:T(8,128)(2,1)} custom-call(bf16[3,128,8,128]{3,2,1,0:T(8,128)(2,1)S(1)} %get-tuple-element.8.y_ref, f32[3,512,2048]{2,1,0:T(8,128)S(1)} %get-tuple-element.9.local_ref, bf16[256,2048]{1,0:T(8,128)(2,1)S(1)} %get-tuple-element.10.back_ref), custom_call_target="tpu_custom_call" | custom-call | tf_op jit(solution)/shard_map/field_part/pallas_call | solution.py:568

commit v3 on v2

--- a/solution.py
+++ b/solution.py
@@ -130,10 +130,9 @@
     def outer_peer(i):
         return lax.rem(z + i, outer)
 
-    h_copies = [
-        pltpu.make_async_copy(h_ref.at[pl.ds(i * block, block)], h_buf.at[i], h_sem.at[i])
-        for i in range(chunks)
-    ]
+    def h_copy(i):
+        return pltpu.make_async_copy(h_ref.at[pl.ds(i * block, block)], h_buf.at[i], h_sem.at[i])
+
     lon_copy = pltpu.make_async_copy(lon_ref, lon_buf, table_sem.at[0])
     local_copy = pltpu.make_async_copy(mixing_ref, local_ref, table_sem.at[4])
     back_copy = pltpu.make_async_copy(back_ref, back_buf, table_sem.at[1])
@@ -145,10 +144,10 @@
         )
         for l in range(layers) for t in range(steps)
     ]
-    h_copies[0].start()
+    h_copy(0).start()
     lon_copy.start()
-    for copy in h_copies[1:]:
-        copy.start()
+    for i in range(1, chunks):
+        h_copy(i).start()
 
     barrier = pltpu.get_barrier_semaphore()
     for i in range(1, group):
@@ -166,26 +165,32 @@
         copy.start()
     back_copy.start()
 
-    parts = [(0, 1, 0, held)] if chunks > 1 else []
-    first_tail = len(parts)
-    parts += [(first_tail, chunks - first_tail, t * outer, outer) for t in range(steps)]
+    early = steps // 2
+
+    def part_of(i, t):
+        if t < early:
+            return i * early + t, i, 1, t
+        return chunks * early + t - early, 0, chunks, t
+
+    def parts_of(t):
+        return [part_of(i, t) for i in range(chunks if t < early else 1)]
 
     def a_copy(part, i):
         to = inner_peer(i)
-        c0, nc, m0, nm = parts[part]
+        slot, c0, nc, t = part
         return pltpu.make_async_remote_copy(
-            src_ref=x_buf.at[pl.ds(c0, nc), pl.ds(to * held + m0, nm)],
-            dst_ref=r_buf.at[pl.ds(c0, nc), s, pl.ds(m0, nm)],
-            send_sem=a_send.at[part, i], recv_sem=a_recv.at[part, i],
+            src_ref=x_buf.at[pl.ds(c0, nc), pl.ds(to * held + t * outer, outer)],
+            dst_ref=r_buf.at[pl.ds(c0, nc), s, pl.ds(t * outer, outer)],
+            send_sem=a_send.at[slot, i], recv_sem=a_recv.at[slot, i],
             device_id={"lat": z * group + to}, device_id_type=MESH,
         )
 
     def own_in(part):
-        c0, nc, m0, nm = parts[part]
+        slot, c0, nc, t = part
         return pltpu.make_async_copy(
-            x_buf.at[pl.ds(c0, nc), pl.ds(s * held + m0, nm)],
-            r_buf.at[pl.ds(c0, nc), s, pl.ds(m0, nm)],
-            own_in_sem.at[part],
+            x_buf.at[pl.ds(c0, nc), pl.ds(s * held + t * outer, outer)],
+            r_buf.at[pl.ds(c0, nc), s, pl.ds(t * outer, outer)],
+            own_in_sem.at[slot],
         )
 
     def b_copy(t, i):
@@ -261,15 +266,15 @@
             a_copy(part, i).start()
 
     def send_head(i):
-        if first_tail:
-            pl.when(i == 0)(lambda: send_part(0))
+        for t in range(early):
+            send_part(part_of(i, t))
 
     def send_tail():
-        for part in range(first_tail, len(parts)):
-            send_part(part)
+        for t in range(early, steps):
+            send_part(part_of(0, t))
 
     def forward(t):
-        for part in ([0] if t == 0 and first_tail else []) + [first_tail + t]:
+        for part in parts_of(t):
             own_in(part).wait()
             for i in range(1, group):
                 a_copy(part, i).wait_recv()
@@ -371,9 +376,10 @@
             d_copy(slot, c0, nc, t, i).wait_recv()
 
     def lat_sent():
-        for part in range(len(parts)):
-            for i in range(1, group):
-                a_copy(part, i).wait_send()
+        for t in range(steps):
+            for part in parts_of(t):
+                for i in range(1, group):
+                    a_copy(part, i).wait_send()
         for t in range(steps):
             if relay:
                 pl.when(at_end)(lambda: f_copy(t).wait_send())
@@ -416,18 +422,13 @@
             landed(*part)
         lat_sent()
 
-    h_copies[0].wait()
     lon_copy.wait()
 
     @pl.loop(0, chunks)
     def _(i):
+        h_copy(i).wait()
         lon_block(i)
-
-        @pl.when(i == 0)
-        def _():
-            pl.semaphore_wait(barrier, group - 1 + outer - 1)
-            for copy in h_copies[1:]:
-                copy.wait()
+        pl.when(i == 0)(lambda: pl.semaphore_wait(barrier, group - 1 + outer - 1))
         send_head(i)
 
     send_tail()
@@ -489,7 +490,7 @@
         jax.ShapeDtypeStruct((chunks, ROW_BLOCK * channels, lon_count), jnp.float32),
         jax.ShapeDtypeStruct(back.shape, bf16),
     ]
-    part_count = steps + (1 if chunks > 1 else 0)
+    part_count = chunks * (steps // 2) + steps - steps // 2
     slots = steps - 1 + chunks
     operands = [
         pltpu.with_memory_space_constraint(a, pltpu.HBM)
@@ -585,7 +586,7 @@
     row_count, channels, lon_count = fields.shape
     layer_count, mode_rows = spectral_weight.shape[:2]
     devices = lax.axis_size("lat")
-    group = math.gcd(devices, 8)
+    group = math.gcd(devices, 16)
     table = lon_table(lon_count, mode_rows)
     forward_lon = jnp.asarray(
         (table / math.sqrt(lon_count)).reshape(lon_count, 2 * mode_rows), jnp.bfloat16

time: 83.4 us -> 77 us (0.923); the launches traced: 83.2 us -> 75.7 us
  Pallas kernels: 83.2 us -> 75.7 us
    pallas_call x1, Pallas kernels: 77.6 us -> 70.1 us  [net_part(): pl.pallas_call(functools.partial(net_kernel, layers, group, outer, steps,...]
where the time goes in v3:
time: 77 us; the launch traced here: 75.7 us
  Pallas kernels  75.7 us (98%)
    pallas_call x1, Pallas kernels, net_part(): pl.pallas_call(functools.partial(net_kernel, layers, group, outer, steps,...  70.1 us
    pallas_call x1, Pallas kernels, field_part(): pl.pallas_call(field_kernel, out_shape=jax.ShapeDtypeStruct((chunks * row...  5.62 us

profile of v3, /device:TPU:0, one launch (start us, length us, event | category | flops | bytes accessed | tf_op | source)
XLA Modules:
  0.0 75.7 jit_solution(14775229512351720331)
XLA Ops:
  0.0 70.1 %net_part.1 = (bf16[3,128,8,128]{3,2,1,0:T(8,128)(2,1)S(1)}, f32[3,512,2048]{2,1,0:T(8,128)S(1)}, bf16[256,2048]{1,0:T(8,128)(2,1)S(1)}) custom-call(bf16[24,64,2048]{2,1,0:T(8,128)(2,1)} %h_ref.1, bf16[2,128,64,128]{3,2,1,0:T(8,128)(2,1)} %weight_ref.1, bf16[2,128,768]{2,1,0:T(8,128)(2,1)} %constant.10.clone.fwd_ref, ...), custom_call_target="tpu_custom_call" | custom-call | tf_op jit(solution)/shard_map/net_part/pallas_call | solution.py:499
  70.1 5.6 %field_part.1 = bf16[24,64,2048]{2,1,0:T(8,128)(2,1)} custom-call(bf16[3,128,8,128]{3,2,1,0:T(8,128)(2,1)S(1)} %get-tuple-element.8.y_ref, f32[3,512,2048]{2,1,0:T(8,128)S(1)} %get-tuple-element.9.local_ref, bf16[256,2048]{1,0:T(8,128)(2,1)S(1)} %get-tuple-element.10.back_ref), custom_call_target="tpu_custom_call" | custom-call | tf_op jit(solution)/shard_map/field_part/pallas_call | solution.py:569

commit v4 on v3

--- a/solution.py
+++ b/solution.py
@@ -11,7 +11,7 @@
 
 KY = 128
 MESH = pl.DeviceIdType.MESH
-LAG = (0, 1, 4, 5, 8)
+LAG = (0, 1, 2, 3, 4)
 ROW_BLOCK = 8
 CHUNK = 512
 NET_VMEM = 20 << 20
@@ -167,29 +167,32 @@
 
     early = steps // 2
 
-    def part_of(i, t):
-        if t < early:
-            return i * early + t, i, 1, t
-        return chunks * early + t - early, 0, chunks, t
+    def early_part(i):
+        return i, i, 1, 0, early * outer
+
+    def late_part(t):
+        return chunks + t - early, 0, chunks, t * outer, outer
 
     def parts_of(t):
-        return [part_of(i, t) for i in range(chunks if t < early else 1)]
+        if t >= early:
+            return [late_part(t)]
+        return [early_part(i) for i in range(chunks)] if t == 0 else []
 
     def a_copy(part, i):
         to = inner_peer(i)
-        slot, c0, nc, t = part
+        slot, c0, nc, m0, nm = part
         return pltpu.make_async_remote_copy(
-            src_ref=x_buf.at[pl.ds(c0, nc), pl.ds(to * held + t * outer, outer)],
-            dst_ref=r_buf.at[pl.ds(c0, nc), s, pl.ds(t * outer, outer)],
+            src_ref=x_buf.at[pl.ds(c0, nc), pl.ds(to * held + m0, nm)],
+            dst_ref=r_buf.at[pl.ds(c0, nc), s, pl.ds(m0, nm)],
             send_sem=a_send.at[slot, i], recv_sem=a_recv.at[slot, i],
             device_id={"lat": z * group + to}, device_id_type=MESH,
         )
 
     def own_in(part):
-        slot, c0, nc, t = part
+        slot, c0, nc, m0, nm = part
         return pltpu.make_async_copy(
-            x_buf.at[pl.ds(c0, nc), pl.ds(s * held + t * outer, outer)],
-            r_buf.at[pl.ds(c0, nc), s, pl.ds(t * outer, outer)],
+            x_buf.at[pl.ds(c0, nc), pl.ds(s * held + m0, nm)],
+            r_buf.at[pl.ds(c0, nc), s, pl.ds(m0, nm)],
             own_in_sem.at[slot],
         )
 
@@ -225,8 +228,7 @@
             own_out_sem.at[slot],
         )
 
-    d_parts = [(t, 0, chunks, t) for t in range(steps - 1)]
-    d_parts += [(steps - 1 + c, c, 1, steps - 1) for c in range(chunks)]
+    d_parts = [(t, 0, chunks, t) for t in range(steps)]
 
     def f_copy(t):
         return pltpu.make_async_remote_copy(
@@ -266,12 +268,12 @@
             a_copy(part, i).start()
 
     def send_head(i):
-        for t in range(early):
-            send_part(part_of(i, t))
+        if early:
+            send_part(early_part(i))
 
     def send_tail():
         for t in range(early, steps):
-            send_part(part_of(0, t))
+            send_part(late_part(t))
 
     def forward(t):
         for part in parts_of(t):
@@ -418,7 +420,7 @@
 
         for name, t in order:
             stages[name](t)
-        for part in d_parts[:steps - 1]:
+        for part in d_parts:
             landed(*part)
         lat_sent()
 
@@ -447,17 +449,12 @@
         def _():
             @pl.loop(0, chunks)
             def _(i):
-                landed(steps - 1 + i, i, 1, steps - 1)
                 spectrum_block(y_ref[i], turn, turned)
                 for first in range(0, block, span):
                     field_rows(first, span, pw_buf.at[i], h_buf.at[i], back_buf, turned)
                 lon_block(i)
                 send_head(i)
 
-        @pl.when(layer == layers - 1)
-        def _():
-            for part in d_parts[steps - 1:]:
-                landed(*part)
         back_sent()
         pl.when(layer < layers - 1)(send_tail)
 
@@ -490,8 +487,8 @@
         jax.ShapeDtypeStruct((chunks, ROW_BLOCK * channels, lon_count), jnp.float32),
         jax.ShapeDtypeStruct(back.shape, bf16),
     ]
-    part_count = chunks * (steps // 2) + steps - steps // 2
-    slots = steps - 1 + chunks
+    part_count = chunks + steps - steps // 2
+    slots = steps
     operands = [
         pltpu.with_memory_space_constraint(a, pltpu.HBM)
         for a in (h, weight, fwd, bwd, lon, back, local)

time: 77 us -> 75.7 us (0.983); the launches traced: 75.7 us -> 75.4 us
  no operation moved by 1% of the time
where the time goes in v4:
time: 75.7 us; the launch traced here: 75.4 us
  Pallas kernels  75.3 us (99%)
    pallas_call x1, Pallas kernels, net_part(): pl.pallas_call(functools.partial(net_kernel, layers, group, outer, steps,...  69.7 us
    pallas_call x1, Pallas kernels, field_part(): pl.pallas_call(field_kernel, out_shape=jax.ShapeDtypeStruct((chunks * row...  5.62 us

profile of v4, /device:TPU:0, one launch (start us, length us, event | category | flops | bytes accessed | tf_op | source)
XLA Modules:
  0.0 75.4 jit_solution(12570740906865608537)
XLA Ops:
  0.0 69.7 %net_part.1 = (bf16[3,128,8,128]{3,2,1,0:T(8,128)(2,1)S(1)}, f32[3,512,2048]{2,1,0:T(8,128)S(1)}, bf16[256,2048]{1,0:T(8,128)(2,1)S(1)}) custom-call(bf16[24,64,2048]{2,1,0:T(8,128)(2,1)} %h_ref.1, bf16[2,128,64,128]{3,2,1,0:T(8,128)(2,1)} %weight_ref.1, bf16[2,128,768]{2,1,0:T(8,128)(2,1)} %constant.10.clone.fwd_ref, ...), custom_call_target="tpu_custom_call" | custom-call | tf_op jit(solution)/shard_map/net_part/pallas_call | solution.py:496
  69.7 5.6 %field_part.1 = bf16[24,64,2048]{2,1,0:T(8,128)(2,1)} custom-call(bf16[3,128,8,128]{3,2,1,0:T(8,128)(2,1)S(1)} %get-tuple-element.8.y_ref, f32[3,512,2048]{2,1,0:T(8,128)S(1)} %get-tuple-element.9.local_ref, bf16[256,2048]{1,0:T(8,128)(2,1)S(1)} %get-tuple-element.10.back_ref), custom_call_target="tpu_custom_call" | custom-call | tf_op jit(solution)/shard_map/field_part/pallas_call | solution.py:566
